TPU v7x, 32 devices: a whole 2x2x4 slice. The times are simulated.
32 devices in a mesh: dp: 4 (over y, x), seq: 8 (over z, core).
Axes of the slice: x: 2, y: 2, z: 4, core: 2. Of those that a mesh axis runs over, the one named last changes fastest.
Arguments:
- inputs: bfloat16 [8, 1024, 1280], P('dp', 'seq'), may hold values from -6 to 6
- cotangent: bfloat16 [8, 1024, 1280], P('dp', 'seq'), may hold values from -6 to 6
- w_query: bfloat16 [1280, 1280], P(('dp', 'seq')), may hold values from -0.15625 to 0.15625
- w_key: bfloat16 [1280, 1280], P(('dp', 'seq')), may hold values from -0.15625 to 0.15625
- w_value: bfloat16 [1280, 1280], P(('dp', 'seq')), may hold values from -0.15625 to 0.15625
- w_out: bfloat16 [1280, 1280], P(('dp', 'seq')), may hold values from -1.25 to 1.25
- w_up: bfloat16 [1280, 1280], P(('dp', 'seq')), may hold values from -0.15625 to 0.15625
- w_down: bfloat16 [1280, 1280], P(('dp', 'seq')), may hold values from -0.15625 to 0.15625
- norm_attn: bfloat16 [1280], P(('dp', 'seq')), may hold values from 0.5 to 1.5
- norm_mlp: bfloat16 [1280], P(('dp', 'seq')), may hold values from 0.5 to 1.5
- query_scale: bfloat16 [1280], P(('dp', 'seq')), may hold values from 0 to 1.5
Outputs:
- output: bfloat16 [8, 1024, 1280], P('dp', 'seq')
- input_grad: float32 [8, 1024, 1280], P('dp', 'seq')
- grad_query: float32 [1280, 1280], P(('dp', 'seq'))
- grad_key: float32 [1280, 1280], P(('dp', 'seq'))
- grad_value: float32 [1280, 1280], P(('dp', 'seq'))
- grad_out: float32 [1280, 1280], P(('dp', 'seq'))
- grad_up: float32 [1280, 1280], P(('dp', 'seq'))
- grad_down: float32 [1280, 1280], P(('dp', 'seq'))
- grad_norm_attn: float32 [1280], P(('dp', 'seq'))
- grad_norm_mlp: float32 [1280], P(('dp', 'seq'))
- grad_query_scale: float32 [1280], P(('dp', 'seq'))
All inputs are finite; a program needn't handle non-finite values.
Results may differ from a plain program's by a relative error of at most 0.014.
Values may be sent and summed in bfloat16 or wider, within the bound.
No kernel may reach another device: no remote copies, remote signals or barrier semaphores. Data moves between devices by JAX's collectives and lax.ppermute only.
A program may use at most 320 MiB of HBM per device.

v0:
```python
import math
import jax
import jax.numpy as jnp
from jax import lax
from jax.sharding import PartitionSpec as P

H = 16
EPS = 1e-06
SOFT_BASE = 1.442695


def weight_outer(left, right):
    return lax.dot_general(
        left, right, (((0,), (0,)), ((), ())), preferred_element_type=jnp.float32
    )


def times_transpose(left, right):
    return lax.dot_general(
        left, right, (((1,), (1,)), ((), ())), preferred_element_type=jnp.float32
    )


def norm_back(grad, normed, inverse, gain):
    scaled = grad * gain
    inner = jnp.mean(scaled * normed, axis=-1, keepdims=True)
    return (inverse * (scaled - normed * inner), jnp.sum(grad * normed, axis=0))


def attend(q_low, k_low, v_low, first_row, num_heads):
    group_rows, model_width = q_low.shape
    head_size = model_width // num_heads
    query_heads = q_low.reshape(group_rows, num_heads, head_size)
    query_place = first_row + lax.iota(jnp.int32, group_rows)
    start_state = (
        jnp.full((num_heads, group_rows), -1e30, jnp.float32),
        jnp.zeros((num_heads, group_rows), jnp.float32),
        jnp.zeros((group_rows, model_width), jnp.float32),
    )
    key_piece = lax.all_gather(k_low, "seq", axis=0, tiled=True)
    value_piece = lax.all_gather(v_low, "seq", axis=0, tiled=True)
    count = key_piece.shape[0]

    def attend_compute(state):
        best, total, accum = state
        key_heads = key_piece.reshape(count, num_heads, head_size)
        value_heads = value_piece.reshape(count, num_heads, head_size)
        scores = jnp.einsum(
            "qhd,khd->hqk", query_heads, key_heads, preferred_element_type=jnp.float32
        )
        key_place = lax.iota(jnp.int32, count)
        allowed = (key_place[None, :] <= query_place[:, None])[None]
        scores = jnp.where(allowed, scores, -1e30)
        fresh = jnp.maximum(best, jnp.max(scores, axis=2))
        shrink = jnp.exp(best - fresh)
        probs = jnp.where(allowed, jnp.exp(scores - fresh[:, :, None]), 0.0)
        total = jnp.sum(probs, axis=2)
        mixed = jnp.einsum(
            "hqk,khd->qhd",
            probs.astype(jnp.bfloat16),
            value_heads,
            preferred_element_type=jnp.float32,
        )
        factor = jnp.repeat(shrink.T, head_size, axis=1)
        return (fresh, total, accum * factor + mixed.reshape(group_rows, model_width))

    best, total, accum = lax.cond(
        jnp.int32(0) > first_row + group_rows - 1, lambda state: state, attend_compute, start_state
    )
    mixed = accum / jnp.repeat(total.T, head_size, axis=1)
    return (mixed, best + jnp.log(total))


def query_grads(q_low, d_mixed, k_low, v_low, log_total, row_delta, first_row, num_heads):
    group_rows, model_width = q_low.shape
    head_size = model_width // num_heads
    query_heads = q_low.reshape(group_rows, num_heads, head_size)
    grad_heads = d_mixed.reshape(group_rows, num_heads, head_size)
    query_place = first_row + lax.iota(jnp.int32, group_rows)
    empty = jnp.zeros((group_rows, model_width), jnp.float32)
    key_piece = lax.all_gather(k_low, "seq", axis=0, tiled=True)
    value_piece = lax.all_gather(v_low, "seq", axis=0, tiled=True)
    count = key_piece.shape[0]

    def query_compute(accum):
        key_heads = key_piece.reshape(count, num_heads, head_size)
        value_heads = value_piece.reshape(count, num_heads, head_size)
        scores = jnp.einsum(
            "qhd,khd->hqk", query_heads, key_heads, preferred_element_type=jnp.float32
        )
        key_place = lax.iota(jnp.int32, count)
        allowed = (key_place[None, :] <= query_place[:, None])[None]
        probs = jnp.where(allowed, jnp.exp(scores - log_total[:, :, None]), 0.0)
        d_prob = jnp.einsum(
            "qhd,khd->hqk", grad_heads, value_heads, preferred_element_type=jnp.float32
        )
        d_score = (probs * (d_prob - row_delta[:, :, None])).astype(jnp.bfloat16)
        added = jnp.einsum("hqk,khd->qhd", d_score, key_heads, preferred_element_type=jnp.float32)
        return added.reshape(group_rows, model_width)

    return lax.cond(
        jnp.int32(0) > first_row + group_rows - 1, lambda accum: accum, query_compute, empty
    )


def key_grads(k_low, v_low, q_low, d_mixed, total_all, delta_all, first_row, num_heads):
    group_rows, model_width = k_low.shape
    head_size = model_width // num_heads
    key_heads = k_low.reshape(group_rows, num_heads, head_size)
    value_heads = v_low.reshape(group_rows, num_heads, head_size)
    key_place = first_row + lax.iota(jnp.int32, group_rows)
    empty = jnp.zeros((group_rows, model_width), jnp.float32)
    query_piece = lax.all_gather(q_low, "seq", axis=0, tiled=True)
    grad_piece = lax.all_gather(d_mixed, "seq", axis=0, tiled=True)
    count = query_piece.shape[0]

    def key_compute(state):
        query_heads = query_piece.reshape(count, num_heads, head_size)
        grad_heads = grad_piece.reshape(count, num_heads, head_size)
        scores = jnp.einsum(
            "qhd,khd->hqk", query_heads, key_heads, preferred_element_type=jnp.float32
        )
        query_place = lax.iota(jnp.int32, count)
        allowed = (key_place[None, :] <= query_place[:, None])[None]
        probs = jnp.where(allowed, jnp.exp(scores - total_all[:, :, None]), 0.0)
        d_prob = jnp.einsum(
            "qhd,khd->hqk", grad_heads, value_heads, preferred_element_type=jnp.float32
        )
        d_score = (probs * (d_prob - delta_all[:, :, None])).astype(jnp.bfloat16)
        more_values = jnp.einsum(
            "hqk,qhd->khd",
            probs.astype(jnp.bfloat16),
            grad_heads,
            preferred_element_type=jnp.float32,
        )
        more_keys = jnp.einsum(
            "hqk,qhd->khd", d_score, query_heads, preferred_element_type=jnp.float32
        )
        return (
            more_keys.reshape(group_rows, model_width),
            more_values.reshape(group_rows, model_width),
        )

    return lax.cond(
        jnp.int32(0) + count - 1 < first_row, lambda state: state, key_compute, (empty, empty)
    )


def per_device(
    inputs,
    cotangent,
    w_query,
    w_key,
    w_value,
    w_out,
    w_up,
    w_down,
    norm_attn,
    norm_mlp,
    query_scale,
):
    micro_count, group_rows, model_width = inputs.shape
    num_heads = H
    head_size = model_width // num_heads
    first_row = lax.axis_index("seq") * group_rows
    results = []
    in_grads = []
    totals = None
    for micro_index in range(micro_count):
        gathered = (
            lax.all_gather(w_query, ("dp", "seq"), axis=0, tiled=True),
            lax.all_gather(w_key, ("dp", "seq"), axis=0, tiled=True),
            lax.all_gather(w_value, ("dp", "seq"), axis=0, tiled=True),
            lax.all_gather(w_out, ("dp", "seq"), axis=0, tiled=True),
            lax.all_gather(w_up, ("dp", "seq"), axis=0, tiled=True),
            lax.all_gather(w_down, ("dp", "seq"), axis=0, tiled=True),
            lax.all_gather(norm_attn, ("dp", "seq"), axis=0, tiled=True),
            lax.all_gather(norm_mlp, ("dp", "seq"), axis=0, tiled=True),
            lax.all_gather(query_scale, ("dp", "seq"), axis=0, tiled=True),
        )
        full_query, full_key, full_value, full_out, full_up, full_down = gathered[:6]
        gain_attn = gathered[6].astype(jnp.float32)
        gain_mlp = gathered[7].astype(jnp.float32)
        scale_param = gathered[8].astype(jnp.float32)
        scale = jax.nn.softplus(scale_param) * (SOFT_BASE / math.sqrt(head_size))
        layer_in = inputs[micro_index].astype(jnp.float32)
        inv_attn = lax.rsqrt(jnp.mean(layer_in * layer_in, axis=-1, keepdims=True) + EPS)
        normed_attn = layer_in * inv_attn
        h_attn = (normed_attn * gain_attn).astype(jnp.bfloat16)
        q_raw = jnp.dot(h_attn, full_query, preferred_element_type=jnp.float32)
        q_low = (q_raw * scale).astype(jnp.bfloat16)
        k_low = jnp.dot(h_attn, full_key, preferred_element_type=jnp.float32).astype(jnp.bfloat16)
        v_low = jnp.dot(h_attn, full_value, preferred_element_type=jnp.float32).astype(jnp.bfloat16)
        mixed, log_total = attend(q_low, k_low, v_low, first_row, num_heads)
        attn_in = mixed.astype(jnp.bfloat16)
        resid = layer_in + jnp.dot(attn_in, full_out, preferred_element_type=jnp.float32)
        inv_mlp = lax.rsqrt(jnp.mean(resid * resid, axis=-1, keepdims=True) + EPS)
        normed_mlp = resid * inv_mlp
        h_mlp = (normed_mlp * gain_mlp).astype(jnp.bfloat16)
        up_proj = jnp.dot(h_mlp, full_up, preferred_element_type=jnp.float32)
        activated = jax.nn.silu(up_proj).astype(jnp.bfloat16)
        layer_out = resid + jnp.dot(activated, full_down, preferred_element_type=jnp.float32)
        results.append(layer_out.astype(jnp.bfloat16))
        regathered = (
            lax.all_gather(w_query, ("dp", "seq"), axis=0, tiled=True),
            lax.all_gather(w_key, ("dp", "seq"), axis=0, tiled=True),
            lax.all_gather(w_value, ("dp", "seq"), axis=0, tiled=True),
            lax.all_gather(w_out, ("dp", "seq"), axis=0, tiled=True),
            lax.all_gather(w_up, ("dp", "seq"), axis=0, tiled=True),
            lax.all_gather(w_down, ("dp", "seq"), axis=0, tiled=True),
        )
        back_query, back_key, back_value, back_out, back_up, back_down = regathered
        cotan_rows = cotangent[micro_index]
        cotan_float = cotan_rows.astype(jnp.float32)
        grad_down = weight_outer(activated, cotan_rows)
        d_act = times_transpose(cotan_rows, back_down)
        sigmoid_up = jax.nn.sigmoid(up_proj)
        d_up = (d_act * sigmoid_up * (1.0 + up_proj * (1.0 - sigmoid_up))).astype(jnp.bfloat16)
        grad_up = weight_outer(h_mlp, d_up)
        d_hmlp = times_transpose(d_up, back_up)
        d_norm_mlp, grad_gain_mlp = norm_back(d_hmlp, normed_mlp, inv_mlp, gain_mlp)
        d_resid = cotan_float + d_norm_mlp
        resid_low = d_resid.astype(jnp.bfloat16)
        grad_out = weight_outer(attn_in, resid_low)
        d_mixed = times_transpose(resid_low, back_out).astype(jnp.bfloat16)
        row_delta = jnp.sum(
            (d_mixed.astype(jnp.float32) * mixed).reshape(group_rows, num_heads, head_size), axis=2
        ).T
        total_all, delta_all = (
            lax.all_gather(log_total, "seq", axis=1, tiled=True),
            lax.all_gather(row_delta, "seq", axis=1, tiled=True),
        )
        d_qlow = query_grads(
            q_low, d_mixed, k_low, v_low, log_total, row_delta, first_row, num_heads
        )
        d_keys, d_values = key_grads(
            k_low, v_low, q_low, d_mixed, total_all, delta_all, first_row, num_heads
        )
        keys_low = d_keys.astype(jnp.bfloat16)
        values_low = d_values.astype(jnp.bfloat16)
        d_qraw = (d_qlow * scale).astype(jnp.bfloat16)
        grad_scale = (
            jnp.sum(d_qlow * q_raw, axis=0)
            * jax.nn.sigmoid(scale_param)
            * (SOFT_BASE / math.sqrt(head_size))
        )
        grad_query = weight_outer(h_attn, d_qraw)
        grad_key = weight_outer(h_attn, keys_low)
        grad_value = weight_outer(h_attn, values_low)
        d_hattn = (
            times_transpose(d_qraw, back_query)
            + times_transpose(keys_low, back_key)
            + times_transpose(values_low, back_value)
        )
        d_norm_attn, grad_gain_attn = norm_back(d_hattn, normed_attn, inv_attn, gain_attn)
        in_grads.append(d_resid + d_norm_attn)
        grad_part = (
            grad_query,
            grad_key,
            grad_value,
            grad_out,
            grad_up,
            grad_down,
            grad_gain_attn,
            grad_gain_mlp,
            grad_scale,
        )
        if totals is None:
            totals = tuple(grad_part)
        else:
            totals = tuple((earlier + later for earlier, later in zip(totals, grad_part)))
    totals = (
        lax.psum_scatter(totals[0], ("dp", "seq"), scatter_dimension=0, tiled=True),
        lax.psum_scatter(totals[1], ("dp", "seq"), scatter_dimension=0, tiled=True),
        lax.psum_scatter(totals[2], ("dp", "seq"), scatter_dimension=0, tiled=True),
        lax.psum_scatter(totals[3], ("dp", "seq"), scatter_dimension=0, tiled=True),
        lax.psum_scatter(totals[4], ("dp", "seq"), scatter_dimension=0, tiled=True),
        lax.psum_scatter(totals[5], ("dp", "seq"), scatter_dimension=0, tiled=True),
        lax.psum_scatter(totals[6], ("dp", "seq"), scatter_dimension=0, tiled=True),
        lax.psum_scatter(totals[7], ("dp", "seq"), scatter_dimension=0, tiled=True),
        lax.psum_scatter(totals[8], ("dp", "seq"), scatter_dimension=0, tiled=True),
    )
    return (
        jnp.stack(results),
        jnp.stack(in_grads),
        totals[0],
        totals[1],
        totals[2],
        totals[3],
        totals[4],
        totals[5],
        totals[6],
        totals[7],
        totals[8],
    )


def solution(mesh):
    placed = (
        P("dp", "seq", None),
        P("dp", "seq", None),
        P(("dp", "seq"), None),
        P(("dp", "seq"), None),
        P(("dp", "seq"), None),
        P(("dp", "seq"), None),
        P(("dp", "seq"), None),
        P(("dp", "seq"), None),
        P(("dp", "seq")),
        P(("dp", "seq")),
        P(("dp", "seq")),
    )
    return jax.shard_map(
        per_device,
        mesh=mesh,
        in_specs=placed,
        out_specs=(
            P("dp", "seq", None),
            P("dp", "seq", None),
            P(("dp", "seq"), None),
            P(("dp", "seq"), None),
            P(("dp", "seq"), None),
            P(("dp", "seq"), None),
            P(("dp", "seq"), None),
            P(("dp", "seq"), None),
            P(("dp", "seq")),
            P(("dp", "seq")),
            P(("dp", "seq")),
        ),
        check_vma=False,
    )
```

profile of v0, /device:TPU:0, one launch (start us, length us, event | category | flops | bytes accessed | tf_op | source)
XLA Modules:
  0.0 1553.3 jit_solution(6274619430469553487)
XLA Ops:
  12.0 42.2 %all-reduce.7 = (bf16[1280]{0:T(1024)(128)(2,1)S(1)}, bf16[1280]{0:T(1024)(128)(2,1)S(1)}, bf16[1280]{0:T(1024)(128)(2,1)S(1)}) all-reduce(bf16[1280]{0:T(1024)(128)(2,1)S(1)} %dynamic-update-slice, bf16[1280]{0:T(1024)(128)(2,1)S(1)} %dynamic-update-slice.1, ...), channel_id=1, replica_groups=mesh['dp'=4,'seq'=8] {'dp','seq'}, use_global_device_ids=true, to_apply=%add | all-reduce | flops 3840 | bytes 15360
  55.5 17.4 %all-gather.15.cloned.1.call-done = bf16[1280,1280]{1,0:T(8,128)(2,1)} async-done(((bf16[40,1280]{1,0:T(8,128)(2,1)}), bf16[1280,1280]{1,0:T(8,128)(2,1)}) %all-gather.15.cloned.1.call-update) | async-done | bytes 3276816 | tf_op jit(solution)/shard_map/all_gather | solution.py:172
  76.5 57.7 %all-gather.21.cloned.1.call-done = bf16[1280,1280]{1,0:T(8,128)(2,1)} async-done(((bf16[40,1280]{1,0:T(8,128)(2,1)}), bf16[1280,1280]{1,0:T(8,128)(2,1)}) %all-gather.21.cloned.1.call-update) | async-done | bytes 3276816 | tf_op jit(solution)/shard_map/all_gather | solution.py:173
  146.4 48.9 %all-gather.19.cloned.1.call-done = bf16[1280,1280]{1,0:T(8,128)(2,1)} async-done(((bf16[40,1280]{1,0:T(8,128)(2,1)}), bf16[1280,1280]{1,0:T(8,128)(2,1)}) %all-gather.19.cloned.1.call-update) | async-done | bytes 3276816 | tf_op jit(solution)/shard_map/all_gather | solution.py:171
  203.1 26.5 %all-gather.31.cloned.1.call-done = bf16[1024,1280]{1,0:T(8,128)(2,1)} async-done(((bf16[128,1280]{1,0:T(8,128)(2,1)}), bf16[1024,1280]{1,0:T(8,128)(2,1)}) %all-gather.31.cloned.1.call-update) | async-done | bytes 2621456 | tf_op jit(solution)/shard_map/all_gather | solution.py:40
  229.6 34.4 %all-gather.33.cloned.1.call-done = bf16[1024,1280]{1,0:T(8,128)(2,1)} async-done(((bf16[128,1280]{1,0:T(8,128)(2,1)}), bf16[1024,1280]{1,0:T(8,128)(2,1)}) %all-gather.33.cloned.1.call-update) | async-done | bytes 2621456 | tf_op jit(solution)/shard_map/all_gather | solution.py:41
  264.0 18.8 %conditional.7 = (f32[16,128]{1,0:T(8,128)S(1)}, f32[16,128]{1,0:T(8,128)S(1)}, f32[16,128]{1,0:T(8,128)S(1)}, f32[128,1280]{1,0:T(8,128)S(1)}) conditional(s32[]{:T(128)} %convert_element_type.190, (s32[128]{0:T(128)S(1)}, bf16[1024,1280]{1,0:T(8,128)(2,1)}, bf16[128,16,80]{0,2,1:T(8,128)(2,1)}, bf16[1024,1280]{1,0:T(8,128)(2,1)}) %tuple.181, () %tuple.67), branch_computations={%region_7.10_spmd, %region_10.11_spmd} | conditional | flops 692357120 | bytes 87835224 | solution.py:67
  297.8 35.1 %all-gather.23.cloned.1.call-done = bf16[1024,1280]{1,0:T(8,128)(2,1)} async-done(((bf16[128,1280]{1,0:T(8,128)(2,1)}), bf16[1024,1280]{1,0:T(8,128)(2,1)}) %all-gather.23.cloned.1.call-update) | async-done | bytes 2621456 | tf_op jit(solution)/shard_map/all_gather | solution.py:41
  332.9 18.8 %conditional.6 = (f32[16,128]{1,0:T(8,128)S(1)}, f32[16,128]{1,0:T(8,128)S(1)}, f32[16,128]{1,0:T(8,128)S(1)}, f32[128,1280]{1,0:T(8,128)S(1)}) conditional(s32[]{:T(128)} %convert_element_type.190, (s32[128]{0:T(128)S(1)}, bf16[1024,1280]{1,0:T(8,128)(2,1)}, bf16[128,16,80]{0,2,1:T(8,128)(2,1)}, bf16[1024,1280]{1,0:T(8,128)(2,1)}) %tuple.179, () %tuple.65), branch_computations={%region_1.4_spmd, %region_4.5_spmd} | conditional | flops 692357120 | bytes 87835224 | solution.py:67
  355.7 38.4 %all-gather.25.cloned.1.call-done = bf16[1280,1280]{1,0:T(8,128)(2,1)} async-done(((bf16[40,1280]{1,0:T(8,128)(2,1)}), bf16[1280,1280]{1,0:T(8,128)(2,1)}) %all-gather.25.cloned.1.call-update) | async-done | bytes 3276816 | tf_op jit(solution)/shard_map/all_gather | solution.py:174
  397.8 57.5 %all-gather.27.cloned.1.call-done = bf16[1280,1280]{1,0:T(8,128)(2,1)} async-done(((bf16[40,1280]{1,0:T(8,128)(2,1)}), bf16[1280,1280]{1,0:T(8,128)(2,1)}) %all-gather.27.cloned.1.call-update) | async-done | bytes 3276816 | tf_op jit(solution)/shard_map/all_gather | solution.py:175
  458.7 57.6 %all-gather.29.cloned.1.call-done = bf16[1280,1280]{1,0:T(8,128)(2,1)} async-done(((bf16[40,1280]{1,0:T(8,128)(2,1)}), bf16[1280,1280]{1,0:T(8,128)(2,1)}) %all-gather.29.cloned.1.call-update) | async-done | bytes 3276816 | tf_op jit(solution)/shard_map/all_gather | solution.py:176
  542.6 26.9 %conditional.10 = (f32[128,1280]{1,0:T(8,128)S(1)}) conditional(s32[]{:T(128)} %convert_element_type.190, (s32[128]{0:T(128)S(1)}, bf16[1024,1280]{1,0:T(8,128)(2,1)}, bf16[128,16,80]{0,2,1:T(8,128)(2,1)S(1)}, f32[16,128]{1,0:T(8,128)S(1)}, bf16[128,1280]{1,0:T(8,128)(2,1)S(1)}, /*index=5*/bf16[1024,1280]{1,0:T(8,128)(2,1)}, ...), branch_computations={%region_21.22_spmd, %region_22.23_spmd} | conditional | flops 1017249792 | bytes 38683144 | solution.py:101
  569.5 29.7 %conditional.8 = (f32[128,1280]{1,0:T(8,128)}) conditional(s32[]{:T(128)} %convert_element_type.190, (s32[128]{0:T(128)S(1)}, bf16[1024,1280]{1,0:T(8,128)(2,1)}, bf16[128,16,80]{0,2,1:T(8,128)(2,1)}, f32[16,128]{1,0:T(8,128)S(1)}, bf16[128,1280]{1,0:T(8,128)(2,1)}, /*index=5*/bf16[1024,1280]{1,0:T(8,128)(2,1)}, ...), branch_computations={%region_14.15_spmd, %region_15.16_spmd} | conditional | flops 1017249792 | bytes 38683144 | solution.py:101
  624.6 15.4 all_gather.106
  640.0 15.1 all_gather.108
  683.8 35.7 %conditional.11 = (bf16[128,1280]{0,1:T(8,128)(2,1)}, bf16[128,1280]{0,1:T(8,128)(2,1)}) conditional(s32[]{:T(128)} %convert_element_type.218, (s32[128]{0:T(128)S(1)}, bf16[1024,1280]{1,0:T(8,128)(2,1)}, bf16[128,1280]{1,0:T(8,128)(2,1)}, f32[16,1024]{1,0:T(8,128)}, bf16[1024,1280]{1,0:T(8,128)(2,1)}, /*index=5*/bf16[128,1280]{1,0:T(8,128)(2,1)}, ...), branch_computations={%region_23.24_spmd, %region_24.25_spmd} | conditional | flops 1359413248 | bytes 49349136 | solution.py:144
  719.5 32.6 %conditional.9 = (bf16[128,1280]{0,1:T(8,128)(2,1)S(1)}, bf16[128,1280]{0,1:T(8,128)(2,1)S(1)}) conditional(s32[]{:T(128)} %convert_element_type.218, (s32[128]{0:T(128)S(1)}, bf16[1024,1280]{1,0:T(8,128)(2,1)}, bf16[128,1280]{1,0:T(8,128)(2,1)S(1)}, f32[16,1024]{1,0:T(8,128)S(1)}, bf16[1024,1280]{1,0:T(8,128)(2,1)}, ...), branch_computations={%region_16.17_spmd, %region_17.18_spmd} | conditional | flops 1359413248 | bytes 49349136 | solution.py:144
  783.4 39.6 %all-reduce.6 = (f32[1280]{0:T(1024)S(1)}, f32[1280]{0:T(1024)S(1)}, f32[1280]{0:T(1024)S(1)}) all-reduce(f32[1280]{0:T(1024)S(1)} %add.209, f32[1280]{0:T(1024)S(1)} %add.210, f32[1280]{0:T(1024)S(1)} %fusion.131), channel_id=8, replica_groups=mesh['dp'=4,'seq'=8] {'dp','seq'}, use_global_device_ids=true, to_apply=%region_34.35.clone | all-reduce | flops 3840 | bytes 30720
  827.4 125.9 %reduce-scatter.13.cloned.1.call-done = f32[40,1280]{1,0:T(8,128)} async-done(((f32[1280,1280]{1,0:T(8,128)}), f32[40,1280]{1,0:T(8,128)}) %reduce-scatter.13.cloned.1.call-update) | async-done | bytes 204816 | tf_op jit(solution)/shard_map/reduce_scatter | solution.py:276
  953.3 147.9 %reduce-scatter.15.cloned.1.call-done = f32[40,1280]{1,0:T(8,128)} async-done(((f32[1280,1280]{1,0:T(8,128)}), f32[40,1280]{1,0:T(8,128)}) %reduce-scatter.15.cloned.1.call-update) | async-done | bytes 204816 | tf_op jit(solution)/shard_map/reduce_scatter | solution.py:277
  1101.2 147.9 %reduce-scatter.17.cloned.1.call-done = f32[40,1280]{1,0:T(8,128)} async-done(((f32[1280,1280]{1,0:T(8,128)}), f32[40,1280]{1,0:T(8,128)}) %reduce-scatter.17.cloned.1.call-update) | async-done | bytes 204816 | tf_op jit(solution)/shard_map/reduce_scatter | solution.py:278
  1249.1 148.5 %reduce-scatter.9.cloned.1.call-done = f32[40,1280]{1,0:T(8,128)} async-done(((f32[1280,1280]{1,0:T(8,128)}), f32[40,1280]{1,0:T(8,128)}) %reduce-scatter.9.cloned.1.call-update) | async-done | bytes 204816 | tf_op jit(solution)/shard_map/reduce_scatter | solution.py:274
  1397.6 148.6 %reduce-scatter.11.cloned.1.call-done = f32[40,1280]{1,0:T(8,128)} async-done(((f32[1280,1280]{1,0:T(8,128)}), f32[40,1280]{1,0:T(8,128)}) %reduce-scatter.11.cloned.1.call-update) | async-done | bytes 204816 | tf_op jit(solution)/shard_map/reduce_scatter | solution.py:275
  (264 shorter events, 333.2 us)
Async XLA Ops:
  7.2 127.0 %copy-start = (bf16[2,128,1280]{2,1,0:T(8,128)(2,1)S(1)}, bf16[2,128,1280]{2,1,0:T(8,128)(2,1)}, u32[]{:S(2)}) copy-start(bf16[2,128,1280]{2,1,0:T(8,128)(2,1)} %param.23) | copy-start | bytes 1966084
  7.2 65.8 %all-gather.15.cloned.1.call-start = ((), (), s32[]{:S(2)}) async-start(), calls=%async_computation.6 | async-start | bytes 3379200 | tf_op jit(solution)/shard_map/all_gather | solution.py:172
  7.9 126.2 %all-gather.21.cloned.1.call-start = ((), (), s32[]{:S(2)}) async-start(), calls=%async_computation.9 | async-start | bytes 3379200 | tf_op jit(solution)/shard_map/all_gather | solution.py:173
  8.7 186.6 %all-gather.19.cloned.1.call-start = ((), (), s32[]{:S(2)}) async-start(), calls=%async_computation.8 | async-start | bytes 3379200 | tf_op jit(solution)/shard_map/all_gather | solution.py:171
  9.4 220.2 %all-gather.31.cloned.1.call-start = ((), (), s32[]{:S(2)}) async-start(), calls=%async_computation.14 | async-start | bytes 2949120 | tf_op jit(solution)/shard_map/all_gather | solution.py:40
  54.2 92.1 %copy-start.40 = (bf16[1280]{0:T(1024)(128)(2,1)}, bf16[1280]{0:T(1024)(128)(2,1)S(1)}, u32[]{:S(2)}) copy-start(bf16[1280]{0:T(1024)(128)(2,1)S(1)} %get-tuple-element.289) | copy-start | bytes 7684
  76.4 187.6 %all-gather.33.cloned.1.call-start = ((), (), s32[]{:S(2)}) async-start(), calls=%async_computation.15 | async-start | bytes 2949120 | tf_op jit(solution)/shard_map/all_gather | solution.py:41
  137.5 160.3 %all-gather.17.cloned.1.call-start = ((), (), s32[]{:S(2)}) async-start(), calls=%async_computation.7 | async-start | bytes 2949120 | tf_op jit(solution)/shard_map/all_gather | solution.py:40
  140.9 192.1 %all-gather.23.cloned.1.call-start = ((), (), s32[]{:S(2)}) async-start(), calls=%async_computation.10 | async-start | bytes 2949120 | tf_op jit(solution)/shard_map/all_gather | solution.py:41
  144.2 250.0 %all-gather.25.cloned.1.call-start = ((), (), s32[]{:S(2)}) async-start(), calls=%async_computation.11 | async-start | bytes 3379200 | tf_op jit(solution)/shard_map/all_gather | solution.py:174
  145.0 310.4 %all-gather.27.cloned.1.call-start = ((), (), s32[]{:S(2)}) async-start(), calls=%async_computation.12 | async-start | bytes 3379200 | tf_op jit(solution)/shard_map/all_gather | solution.py:175
  145.7 370.6 %all-gather.29.cloned.1.call-start = ((), (), s32[]{:S(2)}) async-start(), calls=%async_computation.13 | async-start | bytes 3379200 | tf_op jit(solution)/shard_map/all_gather | solution.py:176
  146.3 537.5 %all-gather.39.cloned.1.call-start = ((), (), s32[]{:S(2)}) async-start(), calls=%async_computation.18 | async-start | bytes 2949120 | tf_op jit(solution)/shard_map/all_gather | solution.py:113
  199.8 64.2 %copy-start.26 = (bf16[128,1280]{1,0:T(8,128)(2,1)}, bf16[128,1280]{1,0:T(8,128)(2,1)S(1)}, u32[]{:S(2)}) copy-start(bf16[128,1280]{1,0:T(8,128)(2,1)S(1)} %get-tuple-element.305) | copy-start | bytes 983044
  199.8 484.0 %all-gather.41.cloned.1.call-start = ((), (), s32[]{:S(2)}) async-start(), calls=%async_computation.19 | async-start | bytes 2949120 | tf_op jit(solution)/shard_map/all_gather | solution.py:114
  354.3 173.0 %copy-start.10 = (f32[128,1280]{1,0:T(8,128)}, f32[128,1280]{1,0:T(8,128)S(1)}, u32[]{:S(2)}) copy-start(f32[128,1280]{1,0:T(8,128)S(1)} %div.48) | copy-start | bytes 1966084
  530.6 188.9 %all-gather.35.cloned.1.call-start = ((), (), s32[]{:S(2)}) async-start(), calls=%async_computation.16 | async-start | bytes 2949120 | tf_op jit(solution)/shard_map/all_gather | solution.py:113
  531.3 188.2 %all-gather.37.cloned.1.call-start = ((), (), s32[]{:S(2)}) async-start(), calls=%async_computation.17 | async-start | bytes 2949120 | tf_op jit(solution)/shard_map/all_gather | solution.py:114
  535.8 291.6 %reduce-scatter.7.cloned.1.call-start = ((), (), s32[]{:S(2)}) async-start(), calls=%async_computation.20 | async-start | bytes 6758400 | tf_op jit(solution)/shard_map/reduce_scatter | solution.py:273
  605.2 348.0 %reduce-scatter.13.cloned.1.call-start = ((), (), s32[]{:S(2)}) async-start(), calls=%async_computation.23 | async-start | bytes 6758400 | tf_op jit(solution)/shard_map/reduce_scatter | solution.py:276
  611.4 489.8 %reduce-scatter.15.cloned.1.call-start = ((), (), s32[]{:S(2)}) async-start(), calls=%async_computation.24 | async-start | bytes 6758400 | tf_op jit(solution)/shard_map/reduce_scatter | solution.py:277
  617.4 631.8 %reduce-scatter.17.cloned.1.call-start = ((), (), s32[]{:S(2)}) async-start(), calls=%async_computation.25 | async-start | bytes 6758400 | tf_op jit(solution)/shard_map/reduce_scatter | solution.py:278
  624.5 773.1 %reduce-scatter.9.cloned.1.call-start = ((), (), s32[]{:S(2)}) async-start(), calls=%async_computation.21 | async-start | bytes 6758400 | tf_op jit(solution)/shard_map/reduce_scatter | solution.py:274
  758.2 788.1 %reduce-scatter.11.cloned.1.call-start = ((), (), s32[]{:S(2)}) async-start(), calls=%async_computation.22 | async-start | bytes 6758400 | tf_op jit(solution)/shard_map/reduce_scatter | solution.py:275
  (40 other events, 253.7 us)
Sparse Core Ops, SparseCore 0:
  10.9 62.0 all-gather.14
  75.8 58.2 all-gather.20
  137.0 58.2 all-gather.18
  196.8 32.7 all-gather.30
  231.1 32.8 all-gather.32
  265.5 32.2 all-gather.16
  299.4 33.4 all-gather.22
  335.8 58.3 all-gather.24
  397.0 58.2 all-gather.26
  458.0 58.2 all-gather.28
  518.0 32.7 all-gather.38
  552.3 32.8 all-gather.40
  586.8 32.8 all-gather.34
  621.2 33.7 all-gather.36
  657.7 147.1 reduce-scatter.6
  807.7 145.5 reduce-scatter.12
  956.0 145.1 reduce-scatter.14
  1103.9 145.1 reduce-scatter.16
  1252.0 145.5 reduce-scatter.8
  1400.3 145.8 reduce-scatter.10
where the time goes:
time: 1560 us; the launch traced here: 1550 us
  waiting for transfers between devices  1110 us (71%)
  matrix products  182 us (12%)
  blocking collectives  141 us (9%)
  local copies, waits for them, and re-layouts  84 us (5%)
  other arithmetic  19.1 us (1%)
    reduce_scatter x1, waiting for transfers between devices, per_device(): lax.psum_scatter(totals[2], ('dp', 'seq'), scatter_dimension=0, tiled=True)  149 us
    reduce_scatter x1, waiting for transfers between devices, per_device(): lax.psum_scatter(totals[1], ('dp', 'seq'), scatter_dimension=0, tiled=True)  148 us
    reduce_scatter x1, waiting for transfers between devices, per_device(): lax.psum_scatter(totals[5], ('dp', 'seq'), scatter_dimension=0, tiled=True)  148 us
    reduce_scatter x1, waiting for transfers between devices, per_device(): lax.psum_scatter(totals[4], ('dp', 'seq'), scatter_dimension=0, tiled=True)  148 us
    reduce_scatter x1, waiting for transfers between devices, per_device(): lax.psum_scatter(totals[3], ('dp', 'seq'), scatter_dimension=0, tiled=True)  126 us
    unnamed x2, blocking collectives  81.8 us
    all_gather x2, waiting for transfers between devices, attend(): value_piece = lax.all_gather(v_low, 'seq', axis=0, tiled=True)  69.5 us
    all_gather x1, waiting for transfers between devices, per_device(): lax.all_gather(w_value, ('dp', 'seq'), axis=0, tiled=True)  57.7 us
  transfers between devices with their start and end apart: 20, of which 15 were waited for; matrix products, arithmetic and copies ran while one was open for 18% of the time, Pallas kernels for 0%

commit v1 on v0

--- a/solution.py
+++ b/solution.py
@@ -37,7 +37,16 @@
         jnp.zeros((num_heads, group_rows), jnp.float32),
         jnp.zeros((group_rows, model_width), jnp.float32),
     )
-    key_piece = lax.all_gather(k_low, "seq", axis=0, tiled=True)
+    w2 = lax.axis_index("seq")
+    extra = lax.axis_size("seq")
+    front, b_now = (extra, w2)
+    key_piece, val = (k_low, 1)
+    while val < front:
+        item_now = lax.ppermute(key_piece, "seq", perm=[(it, it ^ val) for it in range(front)])
+        reply = jnp.concatenate([key_piece, item_now], axis=0)
+        mixed_arr = jnp.concatenate([item_now, key_piece], axis=0)
+        key_piece = jnp.where(b_now & val == 0, reply, mixed_arr)
+        val = 2 * val
     value_piece = lax.all_gather(v_low, "seq", axis=0, tiled=True)
     count = key_piece.shape[0]
 

time: 1560 us -> 1630 us (1.045)
  waiting for transfers between devices: 1110 us -> 1150 us
    ppermute x0 -> x6, waiting for transfers between devices: none -> 104 us  [attend(): lax.ppermute(key_piece, 'seq', perm=[(it, it ^ val) for it in range(front)])]
    all_gather x2, waiting for transfers between devices: 69.5 us -> 0.01 us  [attend(): value_piece = lax.all_gather(v_low, 'seq', axis=0, tiled=True)]
    all_gather x1, waiting for transfers between devices: 57.7 us -> 17.5 us  [per_device(): lax.all_gather(w_value, ('dp', 'seq'), axis=0, tiled=True)]
    all_gather x1, waiting for transfers between devices: 17.4 us -> 52.2 us  [per_device(): lax.all_gather(w_key, ('dp', 'seq'), axis=0, tiled=True)]
    reduce_scatter x1, waiting for transfers between devices: 0.01 us -> 33.3 us  [per_device(): lax.psum_scatter(totals[0], ('dp', 'seq'), scatter_dimension=0, tiled=True)]
    all_gather x1, waiting for transfers between devices: 38.4 us -> 14.6 us  [per_device(): lax.all_gather(w_out, ('dp', 'seq'), axis=0, tiled=True)]
    all_gather x2, waiting for transfers between devices: 39.5 us -> 15.7 us  [query_grads(): key_piece = lax.all_gather(k_low, 'seq', axis=0, tiled=True)]
    reduce_scatter x1, waiting for transfers between devices: 126 us -> 148 us  [per_device(): lax.psum_scatter(totals[3], ('dp', 'seq'), scatter_dimension=0, tiled=True)]
  transfers between devices with their start and end apart: 20 -> 26, of which waited for: 15 -> 19; matrix products, arithmetic and copies ran while one was open for 18% -> 18% of each run, Pallas kernels for 0% -> 0%
where the time goes in v1:
time: 1630 us; the launch traced here: 1620 us
  waiting for transfers between devices  1150 us (71%)
  matrix products  178 us (11%)
  blocking collectives  141 us (9%)
  local copies, waits for them, and re-layouts  97.2 us (6%)
  other arithmetic  31.2 us (2%)
    reduce_scatter x1, waiting for transfers between devices, per_device(): lax.psum_scatter(totals[1], ('dp', 'seq'), scatter_dimension=0, tiled=True)  148 us
    reduce_scatter x1, waiting for transfers between devices, per_device(): lax.psum_scatter(totals[5], ('dp', 'seq'), scatter_dimension=0, tiled=True)  148 us
    reduce_scatter x1, waiting for transfers between devices, per_device(): lax.psum_scatter(totals[3], ('dp', 'seq'), scatter_dimension=0, tiled=True)  148 us
    reduce_scatter x1, waiting for transfers between devices, per_device(): lax.psum_scatter(totals[4], ('dp', 'seq'), scatter_dimension=0, tiled=True)  148 us
    reduce_scatter x1, waiting for transfers between devices, per_device(): lax.psum_scatter(totals[2], ('dp', 'seq'), scatter_dimension=0, tiled=True)  148 us
    ppermute x6, waiting for transfers between devices, attend(): lax.ppermute(key_piece, 'seq', perm=[(it, it ^ val) for it in range(front)])  104 us
    unnamed x2, blocking collectives  81.9 us
    another operation x20, local copies, waits for them, and re-layouts  62.8 us
  transfers between devices with their start and end apart: 26, of which 19 were waited for; matrix products, arithmetic and copies ran while one was open for 18% of the time, Pallas kernels for 0%

profile of v1, /device:TPU:0, one launch (start us, length us, event | category | flops | bytes accessed | tf_op | source)
XLA Modules:
  0.0 1623.5 jit_solution(17894942326029908592)
XLA Ops:
  12.0 42.2 %all-reduce.7 = (bf16[1280]{0:T(1024)(128)(2,1)S(1)}, bf16[1280]{0:T(1024)(128)(2,1)S(1)}, bf16[1280]{0:T(1024)(128)(2,1)S(1)}) all-reduce(bf16[1280]{0:T(1024)(128)(2,1)S(1)} %dynamic-update-slice, bf16[1280]{0:T(1024)(128)(2,1)S(1)} %dynamic-update-slice.1, ...), channel_id=1, replica_groups=mesh['dp'=4,'seq'=8] {'dp','seq'}, use_global_device_ids=true, to_apply=%add | all-reduce | flops 3840 | bytes 15360
  55.5 17.5 %all-gather.19.cloned.1.call-done = bf16[1280,1280]{1,0:T(8,128)(2,1)} async-done(((bf16[40,1280]{1,0:T(8,128)(2,1)}), bf16[1280,1280]{1,0:T(8,128)(2,1)}) %all-gather.19.cloned.1.call-update) | async-done | bytes 3276816 | tf_op jit(solution)/shard_map/all_gather | solution.py:182
  81.9 52.2 %all-gather.15.cloned.1.call-done = bf16[1280,1280]{1,0:T(8,128)(2,1)} async-done(((bf16[40,1280]{1,0:T(8,128)(2,1)}), bf16[1280,1280]{1,0:T(8,128)(2,1)}) %all-gather.15.cloned.1.call-update) | async-done | bytes 3276816 | tf_op jit(solution)/shard_map/all_gather | solution.py:181
  146.2 16.5 %collective-permute-done.4 = bf16[256,1280]{1,0:T(8,128)(2,1)} collective-permute-done((bf16[256,1280]{1,0:T(8,128)(2,1)S(1)}, bf16[256,1280]{1,0:T(8,128)(2,1)}, u32[]{:S(2)}, u32[]{:S(2)}) %collective-permute-start.4) | collective-permute-done | bytes 655392 | tf_op jit(solution)/shard_map/ppermute | solution.py:45
  165.3 27.3 %collective-permute-done.1 = bf16[256,1280]{1,0:T(8,128)(2,1)} collective-permute-done((bf16[256,1280]{1,0:T(8,128)(2,1)S(1)}, bf16[256,1280]{1,0:T(8,128)(2,1)}, u32[]{:S(2)}, u32[]{:S(2)}) %collective-permute-start.1) | collective-permute-done | bytes 655392 | tf_op jit(solution)/shard_map/ppermute | solution.py:45
  195.3 57.0 %all-gather.17.cloned.1.call-done = bf16[1280,1280]{1,0:T(8,128)(2,1)} async-done(((bf16[40,1280]{1,0:T(8,128)(2,1)}), bf16[1280,1280]{1,0:T(8,128)(2,1)}) %all-gather.17.cloned.1.call-update) | async-done | bytes 3276816 | tf_op jit(solution)/shard_map/all_gather | solution.py:180
  270.5 53.7 %collective-permute-done.2 = bf16[512,1280]{1,0:T(8,128)(2,1)} collective-permute-done((bf16[512,1280]{1,0:T(8,128)(2,1)S(1)}, bf16[512,1280]{1,0:T(8,128)(2,1)}, u32[]{:S(2)}, u32[]{:S(2)}) %collective-permute-start.2) | collective-permute-done | bytes 1310752 | tf_op jit(solution)/shard_map/ppermute | solution.py:45
  328.1 23.3 %conditional.7 = (f32[16,128]{1,0:T(8,128)S(1)}, f32[16,128]{1,0:T(8,128)S(1)}, f32[16,128]{1,0:T(8,128)S(1)}, f32[128,1280]{1,0:T(8,128)S(1)}) conditional(s32[]{:T(128)} %convert_element_type.190, (s32[128]{0:T(128)S(1)}, pred[]{:T(512)}, bf16[1024,1280]{1,0:T(8,128)(2,1)}, bf16[1024,1280]{1,0:T(8,128)(2,1)}, bf16[128,16,80]{0,2,1:T(8,128)(2,1)}, ...), branch_computations={%region_7.10_spmd, %region_10.11_spmd} | conditional | flops 693667840 | bytes 102253176 | solution.py:76
  353.4 23.5 %conditional.6 = (f32[16,128]{1,0:T(8,128)S(1)}, f32[16,128]{1,0:T(8,128)S(1)}, f32[16,128]{1,0:T(8,128)S(1)}, f32[128,1280]{1,0:T(8,128)S(1)}) conditional(s32[]{:T(128)} %convert_element_type.190, (s32[128]{0:T(128)S(1)}, pred[]{:T(512)}, bf16[1024,1280]{1,0:T(8,128)(2,1)}, bf16[1024,1280]{1,0:T(8,128)(2,1)}, bf16[128,16,80]{0,2,1:T(8,128)(2,1)}, ...), branch_computations={%region_1.4_spmd, %region_4.5_spmd} | conditional | flops 693667840 | bytes 102253176 | solution.py:76
  399.5 57.5 %all-gather.25.cloned.1.call-done = bf16[1280,1280]{1,0:T(8,128)(2,1)} async-done(((bf16[40,1280]{1,0:T(8,128)(2,1)}), bf16[1280,1280]{1,0:T(8,128)(2,1)}) %all-gather.25.cloned.1.call-update) | async-done | bytes 3276816 | tf_op jit(solution)/shard_map/all_gather | solution.py:184
  460.4 57.7 %all-gather.27.cloned.1.call-done = bf16[1280,1280]{1,0:T(8,128)(2,1)} async-done(((bf16[40,1280]{1,0:T(8,128)(2,1)}), bf16[1280,1280]{1,0:T(8,128)(2,1)}) %all-gather.27.cloned.1.call-update) | async-done | bytes 3276816 | tf_op jit(solution)/shard_map/all_gather | solution.py:185
  552.6 26.7 %conditional.10 = (f32[128,1280]{1,0:T(8,128)S(1)}) conditional(s32[]{:T(128)} %convert_element_type.190, (s32[128]{0:T(128)S(1)}, bf16[1024,1280]{1,0:T(8,128)(2,1)}, bf16[128,16,80]{0,2,1:T(8,128)(2,1)S(1)}, f32[16,128]{1,0:T(8,128)S(1)}, bf16[128,1280]{1,0:T(8,128)(2,1)S(1)}, /*index=5*/bf16[1024,1280]{1,0:T(8,128)(2,1)}, ...), branch_computations={%region_21.22_spmd, %region_22.23_spmd} | conditional | flops 1017249792 | bytes 38683144 | solution.py:110
  587.0 29.7 %conditional.8 = (f32[128,1280]{1,0:T(8,128)}) conditional(s32[]{:T(128)} %convert_element_type.190, (s32[128]{0:T(128)S(1)}, bf16[1024,1280]{1,0:T(8,128)(2,1)}, bf16[128,16,80]{0,2,1:T(8,128)(2,1)}, f32[16,128]{1,0:T(8,128)S(1)}, bf16[128,1280]{1,0:T(8,128)(2,1)}, /*index=5*/bf16[1024,1280]{1,0:T(8,128)(2,1)}, ...), branch_computations={%region_14.15_spmd, %region_15.16_spmd} | conditional | flops 1017249792 | bytes 38683144 | solution.py:110
  642.1 15.5 all_gather.104
  686.6 15.1 all_gather.101
  701.7 32.9 %conditional.11 = (bf16[128,1280]{0,1:T(8,128)(2,1)S(1)}, bf16[128,1280]{0,1:T(8,128)(2,1)}) conditional(s32[]{:T(128)} %convert_element_type.218, (s32[128]{0:T(128)S(1)}, bf16[1024,1280]{1,0:T(8,128)(2,1)}, bf16[128,1280]{1,0:T(8,128)(2,1)S(1)}, f32[16,1024]{1,0:T(8,128)}, bf16[1024,1280]{1,0:T(8,128)(2,1)}, ...), branch_computations={%region_23.24_spmd, %region_24.25_spmd} | conditional | flops 1359413248 | bytes 50659884 | solution.py:153
  734.7 32.7 %conditional.9 = (bf16[128,1280]{0,1:T(8,128)(2,1)S(1)}, bf16[128,1280]{0,1:T(8,128)(2,1)S(1)}) conditional(s32[]{:T(128)} %convert_element_type.218, (s32[128]{0:T(128)S(1)}, bf16[1024,1280]{1,0:T(8,128)(2,1)}, bf16[128,1280]{1,0:T(8,128)(2,1)S(1)}, f32[16,1024]{1,0:T(8,128)S(1)}, bf16[1024,1280]{1,0:T(8,128)(2,1)}, ...), branch_computations={%region_16.17_spmd, %region_17.18_spmd} | conditional | flops 1359413248 | bytes 50659884 | solution.py:153
  798.9 39.7 %all-reduce.6 = (f32[1280]{0:T(1024)S(1)}, f32[1280]{0:T(1024)S(1)}, f32[1280]{0:T(1024)S(1)}) all-reduce(f32[1280]{0:T(1024)S(1)} %add.209, f32[1280]{0:T(1024)S(1)} %add.210, f32[1280]{0:T(1024)S(1)} %fusion.133), channel_id=8, replica_groups=mesh['dp'=4,'seq'=8] {'dp','seq'}, use_global_device_ids=true, to_apply=%region_34.35.clone | all-reduce | flops 3840 | bytes 30720
  842.9 33.3 %reduce-scatter.7.cloned.1.call-done = f32[40,1280]{1,0:T(8,128)} async-done(((f32[1280,1280]{1,0:T(8,128)}), f32[40,1280]{1,0:T(8,128)}) %reduce-scatter.7.cloned.1.call-update) | async-done | bytes 204816 | tf_op jit(solution)/shard_map/reduce_scatter | solution.py:282
  876.2 148.2 %reduce-scatter.13.cloned.1.call-done = f32[40,1280]{1,0:T(8,128)} async-done(((f32[1280,1280]{1,0:T(8,128)}), f32[40,1280]{1,0:T(8,128)}) %reduce-scatter.13.cloned.1.call-update) | async-done | bytes 204816 | tf_op jit(solution)/shard_map/reduce_scatter | solution.py:285
  1024.4 147.7 %reduce-scatter.15.cloned.1.call-done = f32[40,1280]{1,0:T(8,128)} async-done(((f32[1280,1280]{1,0:T(8,128)}), f32[40,1280]{1,0:T(8,128)}) %reduce-scatter.15.cloned.1.call-update) | async-done | bytes 204816 | tf_op jit(solution)/shard_map/reduce_scatter | solution.py:286
  1172.1 148.2 %reduce-scatter.17.cloned.1.call-done = f32[40,1280]{1,0:T(8,128)} async-done(((f32[1280,1280]{1,0:T(8,128)}), f32[40,1280]{1,0:T(8,128)}) %reduce-scatter.17.cloned.1.call-update) | async-done | bytes 204816 | tf_op jit(solution)/shard_map/reduce_scatter | solution.py:287
  1320.3 148.5 %reduce-scatter.9.cloned.1.call-done = f32[40,1280]{1,0:T(8,128)} async-done(((f32[1280,1280]{1,0:T(8,128)}), f32[40,1280]{1,0:T(8,128)}) %reduce-scatter.9.cloned.1.call-update) | async-done | bytes 204816 | tf_op jit(solution)/shard_map/reduce_scatter | solution.py:283
  1468.8 147.6 %reduce-scatter.11.cloned.1.call-done = f32[40,1280]{1,0:T(8,128)} async-done(((f32[1280,1280]{1,0:T(8,128)}), f32[40,1280]{1,0:T(8,128)}) %reduce-scatter.11.cloned.1.call-update) | async-done | bytes 204816 | tf_op jit(solution)/shard_map/reduce_scatter | solution.py:284
  (302 shorter events, 382.8 us)
Async XLA Ops:
  7.2 65.8 %all-gather.19.cloned.1.call-start = ((), (), s32[]{:S(2)}) async-start(), calls=%async_computation.8 | async-start | bytes 3379200 | tf_op jit(solution)/shard_map/all_gather | solution.py:182
  7.9 126.2 %all-gather.15.cloned.1.call-start = ((), (), s32[]{:S(2)}) async-start(), calls=%async_computation.6 | async-start | bytes 3379200 | tf_op jit(solution)/shard_map/all_gather | solution.py:181
  8.7 243.6 %all-gather.17.cloned.1.call-start = ((), (), s32[]{:S(2)}) async-start(), calls=%async_computation.7 | async-start | bytes 3379200 | tf_op jit(solution)/shard_map/all_gather | solution.py:180
  9.4 318.7 %all-gather.29.cloned.1.call-start = ((), (), s32[]{:S(2)}) async-start(), calls=%async_computation.13 | async-start | bytes 2949120 | tf_op jit(solution)/shard_map/all_gather | solution.py:50
  76.4 277.0 %all-gather.21.cloned.1.call-start = ((), (), s32[]{:S(2)}) async-start(), calls=%async_computation.9 | async-start | bytes 2949120 | tf_op jit(solution)/shard_map/all_gather | solution.py:50
  79.8 316.1 %all-gather.23.cloned.1.call-start = ((), (), s32[]{:S(2)}) async-start(), calls=%async_computation.10 | async-start | bytes 3379200 | tf_op jit(solution)/shard_map/all_gather | solution.py:183
  80.4 376.6 %all-gather.25.cloned.1.call-start = ((), (), s32[]{:S(2)}) async-start(), calls=%async_computation.11 | async-start | bytes 3379200 | tf_op jit(solution)/shard_map/all_gather | solution.py:184
  81.1 437.0 %all-gather.27.cloned.1.call-start = ((), (), s32[]{:S(2)}) async-start(), calls=%async_computation.12 | async-start | bytes 3379200 | tf_op jit(solution)/shard_map/all_gather | solution.py:185
  81.9 470.7 %all-gather.37.cloned.1.call-start = ((), (), s32[]{:S(2)}) async-start(), calls=%async_computation.17 | async-start | bytes 2949120 | tf_op jit(solution)/shard_map/all_gather | solution.py:90
  137.5 449.5 %all-gather.31.cloned.1.call-start = ((), (), s32[]{:S(2)}) async-start(), calls=%async_computation.14 | async-start | bytes 2949120 | tf_op jit(solution)/shard_map/all_gather | solution.py:90
  140.9 560.8 %all-gather.39.cloned.1.call-start = ((), (), s32[]{:S(2)}) async-start(), calls=%async_computation.18 | async-start | bytes 2949120 | tf_op jit(solution)/shard_map/all_gather | solution.py:122
  142.8 19.9 %collective-permute-start.4 = (bf16[256,1280]{1,0:T(8,128)(2,1)S(1)}, bf16[256,1280]{1,0:T(8,128)(2,1)}, u32[]{:S(2)}, u32[]{:S(2)}) collective-permute-start(bf16[256,1280]{1,0:T(8,128)(2,1)S(1)} %maximum_select_fusion.3), channel_id=1, source_target_pairs={{0,2},{1,3},{2,0},{3,1},{4,6},{5,7},{6,4},{7,5},{8,10},{9,11},{10,... | collective-permute-start | bytes 1966088 | tf_op jit(solution)/shard_map/ppermute | solution.py:45
  144.9 47.8 %collective-permute-start.1 = (bf16[256,1280]{1,0:T(8,128)(2,1)S(1)}, bf16[256,1280]{1,0:T(8,128)(2,1)}, u32[]{:S(2)}, u32[]{:S(2)}) collective-permute-start(bf16[256,1280]{1,0:T(8,128)(2,1)S(1)} %maximum_select_fusion.2), channel_id=1, source_target_pairs={{0,2},{1,3},{2,0},{3,1},{4,6},{5,7},{6,4},{7,5},{8,10},{9,11},{10,... | collective-permute-start | bytes 1966088 | tf_op jit(solution)/shard_map/ppermute | solution.py:45
  164.3 102.3 %collective-permute-start.5 = (bf16[512,1280]{1,0:T(8,128)(2,1)S(1)}, bf16[512,1280]{1,0:T(8,128)(2,1)}, u32[]{:S(2)}, u32[]{:S(2)}) collective-permute-start(bf16[512,1280]{1,0:T(8,128)(2,1)S(1)} %maximum_select_fusion.1), channel_id=1, source_target_pairs={{0,4},{1,5},{2,6},{3,7},{4,0},{5,1},{6,2},{7,3},{8,12},{9,13},{10,... | collective-permute-start | bytes 3932168 | tf_op jit(solution)/shard_map/ppermute | solution.py:45
  194.6 129.6 %collective-permute-start.2 = (bf16[512,1280]{1,0:T(8,128)(2,1)S(1)}, bf16[512,1280]{1,0:T(8,128)(2,1)}, u32[]{:S(2)}, u32[]{:S(2)}) collective-permute-start(bf16[512,1280]{1,0:T(8,128)(2,1)S(1)} %maximum_select_fusion), channel_id=1, source_target_pairs={{0,4},{1,5},{2,6},{3,7},{4,0},{5,1},{6,2},{7,3},{8,12},{9,13},{10,... | collective-permute-start | bytes 3932168 | tf_op jit(solution)/shard_map/ppermute | solution.py:45
  260.7 441.0 %all-gather.41.cloned.1.call-start = ((), (), s32[]{:S(2)}) async-start(), calls=%async_computation.19 | async-start | bytes 2949120 | tf_op jit(solution)/shard_map/all_gather | solution.py:123
  532.5 202.1 %all-gather.33.cloned.1.call-start = ((), (), s32[]{:S(2)}) async-start(), calls=%async_computation.15 | async-start | bytes 2949120 | tf_op jit(solution)/shard_map/all_gather | solution.py:122
  533.3 201.4 %all-gather.35.cloned.1.call-start = ((), (), s32[]{:S(2)}) async-start(), calls=%async_computation.16 | async-start | bytes 2949120 | tf_op jit(solution)/shard_map/all_gather | solution.py:123
  537.7 338.5 %reduce-scatter.7.cloned.1.call-start = ((), (), s32[]{:S(2)}) async-start(), calls=%async_computation.20 | async-start | bytes 6758400 | tf_op jit(solution)/shard_map/reduce_scatter | solution.py:282
  622.9 401.5 %reduce-scatter.13.cloned.1.call-start = ((), (), s32[]{:S(2)}) async-start(), calls=%async_computation.23 | async-start | bytes 6758400 | tf_op jit(solution)/shard_map/reduce_scatter | solution.py:285
  629.0 543.1 %reduce-scatter.15.cloned.1.call-start = ((), (), s32[]{:S(2)}) async-start(), calls=%async_computation.24 | async-start | bytes 6758400 | tf_op jit(solution)/shard_map/reduce_scatter | solution.py:286
  635.0 685.4 %reduce-scatter.17.cloned.1.call-start = ((), (), s32[]{:S(2)}) async-start(), calls=%async_computation.25 | async-start | bytes 6758400 | tf_op jit(solution)/shard_map/reduce_scatter | solution.py:287
  642.0 826.8 %reduce-scatter.9.cloned.1.call-start = ((), (), s32[]{:S(2)}) async-start(), calls=%async_computation.21 | async-start | bytes 6758400 | tf_op jit(solution)/shard_map/reduce_scatter | solution.py:283
  773.1 843.3 %reduce-scatter.11.cloned.1.call-start = ((), (), s32[]{:S(2)}) async-start(), calls=%async_computation.22 | async-start | bytes 6758400 | tf_op jit(solution)/shard_map/reduce_scatter | solution.py:284
  (54 other events, 722.1 us)
Sparse Core Ops, SparseCore 0:
  10.9 62.0 all-gather.18
  75.8 58.2 all-gather.14
  137.0 115.2 all-gather.16
  253.8 43.4 all-gather.28
  298.8 36.1 all-gather.20
  337.7 58.1 all-gather.22
  398.7 58.2 all-gather.24
  459.9 58.2 all-gather.26
  519.8 32.7 all-gather.36
  554.1 32.8 all-gather.30
  588.7 32.8 all-gather.38
  623.1 33.3 all-gather.40
  658.1 33.5 all-gather.32
  693.2 32.8 all-gather.34
  728.8 147.4 reduce-scatter.6
  879.0 145.3 reduce-scatter.12
  1027.1 144.8 reduce-scatter.14
  1174.8 145.4 reduce-scatter.16
  1323.2 145.5 reduce-scatter.8
  1471.5 144.8 reduce-scatter.10
